TPU v7x, 32 devices: a whole 2x2x4 slice. The times are simulated.
32 devices in a mesh: dom: 8 (over z, y), feat: 4 (over x, core).
Axes of the slice: x: 2, y: 2, z: 4, core: 2. Of those that a mesh axis runs over, the one named last changes fastest.
Arguments:
- feats: bfloat16 [16384, 1024], P('dom', 'feat'), may hold values from -6 to 6
- projection: bfloat16 [1024, 512], P('feat'), may hold values from -0.1875 to 0.1875
- tiles: bfloat16 [1024, 4, 128, 128], P(('dom', 'feat')), may hold values from -0.25 to 0.25
- slot_owner: int32 [1024, 1], P(('dom', 'feat')), may hold values from 0 to 7; in each aligned block of 32 rows (0 to 31, 32 to 63, ...) at most 8 rows name the same one
- slot_block: int32 [1024, 1], P(('dom', 'feat')), may hold values from 0 to 3
- source_block: int32 [1024, 4], P(('dom', 'feat')), may hold values from 0 to 3
- counts: int32 [16384], P(('dom', 'feat')), may hold values from 1 to 4
- out_grad: bfloat16 [16384, 256], P(('dom', 'feat')), may hold values from -0.046875 to 0.046875
Outputs:
- activated: bfloat16 [16384, 256], P(('dom', 'feat'))
- weight_grad: float32 [1024, 512], P('feat')
Inputs may be any that keep to these rules, and one draw needn't show every extreme that they name: `slot_owner`: among the 32 sent rows of one device, no dom index is named more than 8 times; some device names one exactly 8 times.
All inputs are finite; a program needn't handle non-finite values.
Results may differ from a plain program's by a relative error of at most 0.0059.
Values may be sent and summed in bfloat16 or wider, within the bound.
No kernel may reach another device: no remote copies, remote signals or barrier semaphores. Data moves between devices by JAX's collectives and lax.ppermute only.
A program may use at most 128 MiB of HBM per device.

v0:
```python
import jax
import jax.numpy as jnp
from jax import lax
from jax.sharding import PartitionSpec as P


def local(feats, projection, tiles, slot_owner, slot_block, source_block, counts, out_grad):
    tile_size = tiles.shape[-1]
    slot_count = tiles.shape[0]
    per_slot = tiles.shape[1]
    out_width = out_grad.shape[1]
    node_rows = out_grad.shape[0]
    block_count = node_rows // tile_size
    dom_count = lax.axis_size("dom")
    capacity = max(2, 2 * slot_count // dom_count)
    flat_width = tile_size * out_width
    own_rows = lax.all_to_all(feats, "feat", split_axis=0, concat_axis=1, tiled=True)
    full_weight = lax.all_gather(projection, "feat", axis=0, tiled=True)
    projected = jnp.dot(own_rows, full_weight, preferred_element_type=jnp.float32).astype(
        jnp.bfloat16
    )
    neighbour = projected[:, :out_width].reshape(block_count, tile_size, out_width)
    self_part = projected[:, out_width:]
    picked = neighbour[source_block]
    contribution = jnp.einsum("skij,skjh->sih", tiles, picked, preferred_element_type=jnp.float32)
    contribution = contribution.astype(jnp.bfloat16).reshape(slot_count, flat_width)
    slot_dest = slot_owner[:, 0]
    dest_block = slot_block[:, 0]
    dest_hot = (slot_dest[:, None] == jnp.arange(dom_count, dtype=jnp.int32)[None, :]).astype(
        jnp.int32
    )
    before = jnp.cumsum(dest_hot, axis=0) - dest_hot
    position = jnp.sum(before * dest_hot, axis=1)
    slot_index = slot_dest * capacity + position
    placing = jnp.arange(dom_count * capacity, dtype=jnp.int32)[:, None] == slot_index[None, :]
    outgoing = jnp.dot(
        placing.astype(jnp.bfloat16), contribution, preferred_element_type=jnp.float32
    )
    outgoing = outgoing.astype(jnp.bfloat16).reshape(dom_count, capacity, flat_width)
    labels = jnp.sum(placing.astype(jnp.int32) * (dest_block + 1)[None, :], axis=1) - 1
    labels = labels.reshape(dom_count, capacity)
    incoming, got_labels = (
        lax.all_to_all(outgoing, "dom", split_axis=0, concat_axis=0, tiled=True),
        lax.all_to_all(labels, "dom", split_axis=0, concat_axis=0, tiled=True),
    )
    incoming = incoming.reshape(dom_count * capacity, flat_width)
    receive_hot = (
        jnp.arange(block_count, dtype=jnp.int32)[:, None] == got_labels.reshape(-1)[None, :]
    ).astype(jnp.bfloat16)
    summed = jnp.dot(receive_hot, incoming, preferred_element_type=jnp.float32).reshape(
        node_rows, out_width
    )
    degree = counts.astype(jnp.float32)[:, None]
    preact = summed / degree + self_part.astype(jnp.float32)
    sigma = jax.nn.sigmoid(preact)
    activated = (preact * sigma).astype(jnp.bfloat16)
    grad_pre = out_grad.astype(jnp.float32) * sigma * (1.0 + preact * (1.0 - sigma))
    grad_self = grad_pre.astype(jnp.bfloat16)
    grad_sum = (grad_pre / degree).astype(jnp.bfloat16).reshape(block_count, flat_width)
    sending_back = jnp.dot(receive_hot.T, grad_sum, preferred_element_type=jnp.float32)
    sending_back = sending_back.astype(jnp.bfloat16).reshape(dom_count, capacity, flat_width)
    returned = lax.all_to_all(sending_back, "dom", split_axis=0, concat_axis=0, tiled=True).reshape(
        dom_count * capacity, flat_width
    )
    slot_grad = jnp.dot(
        placing.T.astype(jnp.bfloat16), returned, preferred_element_type=jnp.float32
    )
    slot_grad = slot_grad.astype(jnp.bfloat16).reshape(slot_count, tile_size, out_width)
    products = jnp.einsum("skij,sih->skjh", tiles, slot_grad, preferred_element_type=jnp.float32)
    source_hot = (
        jnp.arange(block_count, dtype=jnp.int32)[:, None] == source_block.reshape(-1)[None, :]
    ).astype(jnp.float32)
    flat_products = products.reshape(slot_count * per_slot, tile_size, out_width)
    grad_neigh = jnp.einsum(
        "bn,njh->bjh", source_hot, flat_products, precision=lax.Precision.HIGHEST
    )
    grad_neigh = grad_neigh.astype(jnp.bfloat16).reshape(node_rows, out_width)
    grad_proj = jnp.concatenate([grad_neigh, grad_self], axis=1)
    partial_grad = lax.psum_scatter(
        lax.dot_general(
            own_rows, grad_proj, (((0,), (0,)), ((), ())), preferred_element_type=jnp.float32
        ),
        "feat",
        scatter_dimension=0,
        tiled=True,
    )
    weight_grad = lax.psum(partial_grad, "dom")
    return (activated, weight_grad)


def solution(mesh):
    placed = (
        P("dom", "feat"),
        P("feat", None),
        P(("dom", "feat"), None, None, None),
        P(("dom", "feat"), None),
        P(("dom", "feat"), None),
        P(("dom", "feat"), None),
        P(("dom", "feat")),
        P(("dom", "feat"), None),
    )
    return jax.shard_map(
        local,
        mesh=mesh,
        in_specs=placed,
        out_specs=(P(("dom", "feat"), None), P("feat", None)),
        check_vma=False,
    )
```

profile of v0, /device:TPU:0, one launch (start us, length us, event | category | flops | bytes accessed | tf_op | source)
XLA Modules:
  0.0 421.0 jit_solution(1731139456741465177)
XLA Ops:
  7.9 4.2 %all-to-all-start.1 = ((bf16[4,512,256]{2,1,0:T(8,128)(2,1)}), bf16[4,512,256]{2,1,0:T(8,128)(2,1)S(1)}, u32[]{:S(2)}, u32[]{:S(2)}) async-start(bf16[4,512,256]{2,1,0:T(8,128)(2,1)} %bitcast.67), calls=%async_computation.1 | async-start | bytes 2097152 | tf_op jit(solution)/shard_map/all_to_all | solution.py:17
  14.5 0.8 select_reduce_fusion.1
  16.8 15.2 %all-to-all-done.1 = bf16[4,512,256]{2,1,0:T(8,128)(2,1)S(1)} async-done(((bf16[4,512,256]{2,1,0:T(8,128)(2,1)}), bf16[4,512,256]{2,1,0:T(8,128)(2,1)S(1)}, u32[]{:S(2)}, u32[]{:S(2)}) %all-to-all-start.1) | async-done | bytes 1048608 | tf_op jit(solution)/shard_map/all_to_all | solution.py:17
  32.0 6.8 %all-to-all-start = ((s32[8,1,8]{2,1,0:T(1,128)}), s32[8,1,8]{2,1,0:T(1,128)S(1)}, u32[]{:S(2)}, u32[]{:S(2)}) async-start(s32[8,1,8]{2,1,0:T(1,128)} %bitcast.2), calls=%async_computation | async-start | bytes 8192 | tf_op jit(solution)/shard_map/all_to_all | solution.py:44
  39.3 2.0 convolution_convert_fusion.3
  41.3 6.5 %gather_fusion = bf16[128,128,256]{2,1,0:T(8,128)(2,1)} fusion(bf16[4,128,256]{2,1,0:T(8,128)(2,1)S(1)} %bitcast.56, s32[1024]{0:T(1024)S(1)} %pad_clamp_fusion), kind=kCustom, calls=%fused_computation | custom fusion | bytes 16777728 | tf_op jit(solution)/shard_map/gather | solution.py:24
  47.8 7.0 %fusion.7 = bf16[32,128,256]{1,2,0:T(8,128)(2,1)S(1)} fusion(bf16[32,4,128,256]{3,2,1,0:T(8,128)(2,1)} %bitcast.58, bf16[32,4,128,128]{3,2,1,0:T(8,128)(2,1)} %param.10), kind=kOutput, calls=%fused_computation.13 | convolution fusion | flops 1074790400 | bytes 14680064 | tf_op jit(solution)/shard_map/skij,skjh->sih/dot_general | solution.py:25
  54.8 2.9 copy.58
  57.7 4.9 %fusion = bf16[8,8,32768]{2,1,0:T(8,128)(2,1)} fusion(bf16[32,32768]{1,0:T(8,128)(2,1)} %bitcast.61, s32[32]{0:T(128)S(1)} %multiply_add_fusion), kind=kOutput, calls=%fused_computation.3 | convolution fusion | flops 136316928 | bytes 6291584 | tf_op jit(solution)/shard_map/dot_general | solution.py:36
  62.6 6.2 %all-to-all-start.2 = ((bf16[8,8,32768]{2,1,0:T(8,128)(2,1)}), bf16[8,8,32768]{2,1,0:T(8,128)(2,1)}, u32[]{:S(2)}, u32[]{:S(2)}) async-start(bf16[8,8,32768]{2,1,0:T(8,128)(2,1)} %fusion), calls=%async_computation.2 | async-start | bytes 8388608 | tf_op jit(solution)/shard_map/all_to_all | solution.py:43
  70.1 90.7 %all-to-all-done.2 = bf16[8,8,32768]{2,1,0:T(8,128)(2,1)} async-done(((bf16[8,8,32768]{2,1,0:T(8,128)(2,1)}), bf16[8,8,32768]{2,1,0:T(8,128)(2,1)}, u32[]{:S(2)}, u32[]{:S(2)}) %all-to-all-start.2) | async-done | bytes 4194336 | tf_op jit(solution)/shard_map/all_to_all | solution.py:43
  160.8 2.8 fusion.3
  164.0 1.1 divide_convert_fusion
  165.3 3.3 fusion.1
  168.6 4.7 %all-to-all-start.3 = ((bf16[8,8,32768]{2,1,0:T(8,128)(2,1)}), bf16[8,8,32768]{2,1,0:T(8,128)(2,1)}, u32[]{:S(2)}, u32[]{:S(2)}) async-start(bf16[8,8,32768]{2,1,0:T(8,128)(2,1)} %fusion.1), calls=%async_computation.3 | async-start | bytes 8388608 | tf_op jit(solution)/shard_map/all_to_all | solution.py:62
  173.7 92.1 %all-to-all-done.3 = bf16[8,8,32768]{2,1,0:T(8,128)(2,1)} async-done(((bf16[8,8,32768]{2,1,0:T(8,128)(2,1)}), bf16[8,8,32768]{2,1,0:T(8,128)(2,1)}, u32[]{:S(2)}, u32[]{:S(2)}) %all-to-all-start.3) | async-done | bytes 4194336 | tf_op jit(solution)/shard_map/all_to_all | solution.py:62
  265.9 3.1 convolution_convert_fusion.2
  269.5 8.1 %fusion.5 = f32[32,256,4,128]{3,1,2,0:T(8,128)} fusion(bf16[32,4,128,128]{3,2,1,0:T(8,128)(2,1)S(1)} %copy-done, bf16[32,128,256]{2,1,0:T(8,128)(2,1)S(1)} %bitcast.62), kind=kOutput, calls=%fused_computation.10 | convolution fusion | flops 1073741824 | bytes 23068672 | tf_op jit(solution)/shard_map/skij,sih->skjh/dot_general | solution.py:69
  277.6 17.6 %copy.51 = f32[128,128,256]{2,0,1:T(8,128)} copy(f32[128,128,256]{1,2,0:T(8,128)} %bitcast.57) | data formatting | bytes 33554432 | tf_op jit(solution)/shard_map/reshape | solution.py:73
  295.2 9.0 %convolution_convert_fusion.4 = bf16[4,128,256]{2,0,1:T(4,128)(2,1)S(1)} fusion(f32[128,128,256]{2,0,1:T(8,128)} %copy.51, s32[128]{0:T(128)S(1)} %eq.67), kind=kOutput, calls=%fused_computation.15 | convolution fusion | flops 201458176 | bytes 17039872 | tf_op jit(solution)/shard_map/bn,njh->bjh/dot_general | solution.py:74
  304.3 2.1 convolution_bitcast_fusion
  306.5 29.7 %reduce-scatter.2.cloned.1.call-done = f32[256,512]{0,1:T(8,128)} async-done(((f32[1024,512]{0,1:T(8,128)}), f32[256,512]{0,1:T(8,128)}) %reduce-scatter.2.cloned.1.call-update) | async-done | bytes 524304 | tf_op jit(solution)/shard_map/reduce_scatter | solution.py:79
  336.2 76.2 %all-reduce.2.cloned.1.call-done = f32[256,512]{0,1:T(8,128)} async-done(((f32[256,512]{0,1:T(8,128)}), f32[256,512]{0,1:T(8,128)}) %all-reduce.2.cloned.1.call-update) | async-done | bytes 524304 | tf_op jit(solution)/shard_map/psum | solution.py:87
  412.5 2.0 copy.53
  (43 shorter events, 7.9 us)
Async XLA Ops:
  7.2 32.2 %all-gather.2.cloned.1.call-start = ((), (), s32[]{:S(2)}) async-start(), calls=%async_computation.5 | async-start | bytes 1310720 | tf_op jit(solution)/shard_map/all_gather | solution.py:18
  7.9 24.1 %all-to-all-start.1 = ((bf16[4,512,256]{2,1,0:T(8,128)(2,1)}), bf16[4,512,256]{2,1,0:T(8,128)(2,1)S(1)}, u32[]{:S(2)}, u32[]{:S(2)}) async-start(bf16[4,512,256]{2,1,0:T(8,128)(2,1)} %bitcast.67), calls=%async_computation.1 | async-start | bytes 2097152 | tf_op jit(solution)/shard_map/all_to_all | solution.py:17
  32.0 30.6 %all-to-all-start = ((s32[8,1,8]{2,1,0:T(1,128)}), s32[8,1,8]{2,1,0:T(1,128)S(1)}, u32[]{:S(2)}, u32[]{:S(2)}) async-start(s32[8,1,8]{2,1,0:T(1,128)} %bitcast.2), calls=%async_computation | async-start | bytes 8192 | tf_op jit(solution)/shard_map/all_to_all | solution.py:44
  41.3 6.5 %copy-start.1 = (bf16[512,512]{1,0:T(8,128)(2,1)}, bf16[512,512]{1,0:T(8,128)(2,1)S(1)}, u32[]{:S(2)}) copy-start(bf16[512,512]{1,0:T(8,128)(2,1)S(1)} %convolution_convert_fusion.3) | copy-start | bytes 1572868
  62.6 6.2 %copy-start.5 = (s32[512]{0:T(512)S(1)}, s32[512]{0:T(512)}, u32[]{:S(2)}) copy-start(s32[512]{0:T(512)} %param.14) | copy-start | bytes 6148
  62.6 98.2 %all-to-all-start.2 = ((bf16[8,8,32768]{2,1,0:T(8,128)(2,1)}), bf16[8,8,32768]{2,1,0:T(8,128)(2,1)}, u32[]{:S(2)}, u32[]{:S(2)}) async-start(bf16[8,8,32768]{2,1,0:T(8,128)(2,1)} %fusion), calls=%async_computation.2 | async-start | bytes 8388608 | tf_op jit(solution)/shard_map/all_to_all | solution.py:43
  68.8 95.2 %copy-start.2 = (bf16[512,512]{1,0:T(8,128)(2,1)S(1)}, bf16[512,512]{1,0:T(8,128)(2,1)}, u32[]{:S(2)}) copy-start(bf16[512,512]{1,0:T(8,128)(2,1)} %copy-done.1) | copy-start | bytes 1572868
  68.8 95.2 %copy-start.3 = (bf16[512,256]{1,0:T(8,128)(2,1)S(1)}, bf16[512,256]{1,0:T(8,128)(2,1)}, u32[]{:S(2)}) copy-start(bf16[512,256]{1,0:T(8,128)(2,1)} %param.15) | copy-start | bytes 786436
  168.6 4.9 %copy-start.4 = (s32[32,4]{0,1:T(4,128)S(1)}, s32[32,4]{0,1:T(4,128)}, u32[]{:S(2)}) copy-start(s32[32,4]{0,1:T(4,128)} %param.13) | copy-start | bytes 1540
  168.6 97.2 %all-to-all-start.3 = ((bf16[8,8,32768]{2,1,0:T(8,128)(2,1)}), bf16[8,8,32768]{2,1,0:T(8,128)(2,1)}, u32[]{:S(2)}, u32[]{:S(2)}) async-start(bf16[8,8,32768]{2,1,0:T(8,128)(2,1)} %fusion.1), calls=%async_computation.3 | async-start | bytes 8388608 | tf_op jit(solution)/shard_map/all_to_all | solution.py:62
  173.3 162.9 %reduce-scatter.2.cloned.1.call-start = ((), (), s32[]{:S(2)}) async-start(), calls=%async_computation.6 | async-start | bytes 2621440 | tf_op jit(solution)/shard_map/reduce_scatter | solution.py:79
  265.9 3.6 copy-start
  306.4 106.1 %all-reduce.2.cloned.1.call-start = ((), (), s32[]{:S(2)}) async-start(), calls=%async_computation.7 | async-start | bytes 1048576 | tf_op jit(solution)/shard_map/psum | solution.py:87
Sparse Core Ops, SparseCore 0:
  9.5 24.1 all-gather.1
  306.5 29.6 reduce-scatter.1
  339.6 72.7 all-reduce.1
where the time goes:
time: 422 us; the launch traced here: 421 us
  waiting for transfers between devices  305 us (72%)
  matrix products  42.3 us (10%)
  local copies, waits for them, and re-layouts  32.4 us (8%)
  starting transfers between devices  22.1 us (5%)
  between operations  13.9 us (3%)
  other arithmetic  5.48 us (1%)
    all_to_all x1, waiting for transfers between devices, local(): lax.all_to_all(sending_back, 'dom', split_axis=0, concat_axis=0, tiled=True)  92.1 us
    all_to_all x1, waiting for transfers between devices, local(): lax.all_to_all(outgoing, 'dom', split_axis=0, concat_axis=0, tiled=True)  90.7 us
    psum x1, waiting for transfers between devices, local(): weight_grad = lax.psum(partial_grad, 'dom')  76.2 us
    reduce_scatter x1, waiting for transfers between devices, local(): lax.psum_scatter(lax.dot_general(own_rows, grad_proj, (((0,), (0,)), ((),...  29.7 us
    reshape x1, local copies, waits for them, and re-layouts, local(): products.reshape(slot_count * per_slot, tile_size, out_width)  17.6 us
    all_to_all x1, waiting for transfers between devices, local(): lax.all_to_all(feats, 'feat', split_axis=0, concat_axis=1, tiled=True)  15.2 us
    dot_general x1, matrix products, local(): jnp.einsum('bn,njh->bjh', source_hot, flat_products, precision=lax.Precis...  9.02 us
  transfers between devices with their start and end apart: 7, of which 5 were waited for; matrix products, arithmetic and copies ran while one was open for 7% of the time, Pallas kernels for 0%

commit v1 on v0

--- a/solution.py
+++ b/solution.py
@@ -84,7 +84,11 @@
         scatter_dimension=0,
         tiled=True,
     )
-    weight_grad = lax.psum(partial_grad, "dom")
+    weight_grad = partial_grad
+    for hop in (1, 2, 4):
+        weight_grad = weight_grad + lax.ppermute(
+            weight_grad, "dom", [(dev, dev ^ hop) for dev in range(8)]
+        )
     return (activated, weight_grad)
 
 

time: 422 us -> 397 us (0.941)
  waiting for transfers between devices: 305 us -> 274 us
  starting transfers between devices: 22.1 us -> 27.6 us
    psum x1 -> x0, waiting for transfers between devices: 76.2 us -> none  [local(): weight_grad = lax.psum(partial_grad, 'dom')]
    ppermute x0 -> x3, waiting for transfers between devices: none -> 44.9 us  [local(): lax.ppermute(weight_grad, 'dom', [(dev, dev ^ hop) for dev in range(8)])]
    ppermute x0 -> x3, starting transfers between devices: none -> 5.48 us  [local(): lax.ppermute(weight_grad, 'dom', [(dev, dev ^ hop) for dev in range(8)])]
  transfers between devices with their start and end apart: 7 -> 9, of which waited for: 5 -> 7; matrix products, arithmetic and copies ran while one was open for 7% -> 8% of each run, Pallas kernels for 0% -> 0%
where the time goes in v1:
time: 397 us; the launch traced here: 396 us
  waiting for transfers between devices  274 us (69%)
  matrix products  42.3 us (11%)
  local copies, waits for them, and re-layouts  31.4 us (8%)
  starting transfers between devices  27.6 us (7%)
  between operations  14.2 us (4%)
  other arithmetic  6.73 us (2%)
    all_to_all x1, waiting for transfers between devices, local(): lax.all_to_all(sending_back, 'dom', split_axis=0, concat_axis=0, tiled=True)  92.1 us
    all_to_all x1, waiting for transfers between devices, local(): lax.all_to_all(outgoing, 'dom', split_axis=0, concat_axis=0, tiled=True)  90.7 us
    ppermute x3, waiting for transfers between devices, local(): lax.ppermute(weight_grad, 'dom', [(dev, dev ^ hop) for dev in range(8)])  44.9 us
    reduce_scatter x1, waiting for transfers between devices, local(): lax.psum_scatter(lax.dot_general(own_rows, grad_proj, (((0,), (0,)), ((),...  29.8 us
    reshape x1, local copies, waits for them, and re-layouts, local(): products.reshape(slot_count * per_slot, tile_size, out_width)  17.7 us
    all_to_all x1, waiting for transfers between devices, local(): lax.all_to_all(feats, 'feat', split_axis=0, concat_axis=1, tiled=True)  15.2 us
    dot_general x1, matrix products, local(): jnp.einsum('bn,njh->bjh', source_hot, flat_products, precision=lax.Precis...  9.02 us
    dot_general x1, matrix products, local(): jnp.einsum('skij,sih->skjh', tiles, slot_grad, preferred_element_type=jnp...  8.11 us
  transfers between devices with their start and end apart: 9, of which 7 were waited for; matrix products, arithmetic and copies ran while one was open for 8% of the time, Pallas kernels for 0%

profile of v1, /device:TPU:0, one launch (start us, length us, event | category | flops | bytes accessed | tf_op | source)
XLA Modules:
  0.0 395.8 jit_solution(4329856704647381211)
XLA Ops:
  7.9 4.2 %all-to-all-start.1 = ((bf16[4,512,256]{2,1,0:T(8,128)(2,1)}), bf16[4,512,256]{2,1,0:T(8,128)(2,1)S(1)}, u32[]{:S(2)}, u32[]{:S(2)}) async-start(bf16[4,512,256]{2,1,0:T(8,128)(2,1)} %bitcast.67), calls=%async_computation.1 | async-start | bytes 2097152 | tf_op jit(solution)/shard_map/all_to_all | solution.py:17
  16.8 15.2 %all-to-all-done.1 = bf16[4,512,256]{2,1,0:T(8,128)(2,1)S(1)} async-done(((bf16[4,512,256]{2,1,0:T(8,128)(2,1)}), bf16[4,512,256]{2,1,0:T(8,128)(2,1)S(1)}, u32[]{:S(2)}, u32[]{:S(2)}) %all-to-all-start.1) | async-done | bytes 1048608 | tf_op jit(solution)/shard_map/all_to_all | solution.py:17
  32.0 6.8 %all-to-all-start = ((s32[8,1,8]{2,1,0:T(1,128)}), s32[8,1,8]{2,1,0:T(1,128)S(1)}, u32[]{:S(2)}, u32[]{:S(2)}) async-start(s32[8,1,8]{2,1,0:T(1,128)} %bitcast.2), calls=%async_computation | async-start | bytes 8192 | tf_op jit(solution)/shard_map/all_to_all | solution.py:44
  39.3 2.0 convolution_convert_fusion.3
  41.3 6.5 %gather_fusion = bf16[128,128,256]{2,1,0:T(8,128)(2,1)} fusion(bf16[4,128,256]{2,1,0:T(8,128)(2,1)S(1)} %bitcast.56, s32[1024]{0:T(1024)S(1)} %pad_clamp_fusion), kind=kCustom, calls=%fused_computation | custom fusion | bytes 16777728 | tf_op jit(solution)/shard_map/gather | solution.py:24
  47.8 7.0 %fusion.7 = bf16[32,128,256]{1,2,0:T(8,128)(2,1)S(1)} fusion(bf16[32,4,128,256]{3,2,1,0:T(8,128)(2,1)} %bitcast.58, bf16[32,4,128,128]{3,2,1,0:T(8,128)(2,1)} %param.10), kind=kOutput, calls=%fused_computation.13 | convolution fusion | flops 1074790400 | bytes 14680064 | tf_op jit(solution)/shard_map/skij,skjh->sih/dot_general | solution.py:25
  54.8 2.9 copy.58
  57.7 4.9 %fusion = bf16[8,8,32768]{2,1,0:T(8,128)(2,1)} fusion(bf16[32,32768]{1,0:T(8,128)(2,1)} %bitcast.61, s32[32]{0:T(128)S(1)} %multiply_add_fusion), kind=kOutput, calls=%fused_computation.3 | convolution fusion | flops 136316928 | bytes 6291584 | tf_op jit(solution)/shard_map/dot_general | solution.py:36
  62.6 6.2 %all-to-all-start.2 = ((bf16[8,8,32768]{2,1,0:T(8,128)(2,1)}), bf16[8,8,32768]{2,1,0:T(8,128)(2,1)}, u32[]{:S(2)}, u32[]{:S(2)}) async-start(bf16[8,8,32768]{2,1,0:T(8,128)(2,1)} %fusion), calls=%async_computation.2 | async-start | bytes 8388608 | tf_op jit(solution)/shard_map/all_to_all | solution.py:43
  70.1 90.7 %all-to-all-done.2 = bf16[8,8,32768]{2,1,0:T(8,128)(2,1)} async-done(((bf16[8,8,32768]{2,1,0:T(8,128)(2,1)}), bf16[8,8,32768]{2,1,0:T(8,128)(2,1)}, u32[]{:S(2)}, u32[]{:S(2)}) %all-to-all-start.2) | async-done | bytes 4194336 | tf_op jit(solution)/shard_map/all_to_all | solution.py:43
  160.8 2.8 fusion.3
  165.3 3.3 fusion.1
  168.6 4.7 %all-to-all-start.3 = ((bf16[8,8,32768]{2,1,0:T(8,128)(2,1)}), bf16[8,8,32768]{2,1,0:T(8,128)(2,1)}, u32[]{:S(2)}, u32[]{:S(2)}) async-start(bf16[8,8,32768]{2,1,0:T(8,128)(2,1)} %fusion.1), calls=%async_computation.3 | async-start | bytes 8388608 | tf_op jit(solution)/shard_map/all_to_all | solution.py:62
  173.7 92.1 %all-to-all-done.3 = bf16[8,8,32768]{2,1,0:T(8,128)(2,1)} async-done(((bf16[8,8,32768]{2,1,0:T(8,128)(2,1)}), bf16[8,8,32768]{2,1,0:T(8,128)(2,1)}, u32[]{:S(2)}, u32[]{:S(2)}) %all-to-all-start.3) | async-done | bytes 4194336 | tf_op jit(solution)/shard_map/all_to_all | solution.py:62
  265.9 3.1 convolution_convert_fusion.2
  269.5 8.1 %fusion.5 = f32[32,256,4,128]{3,1,2,0:T(8,128)} fusion(bf16[32,4,128,128]{3,2,1,0:T(8,128)(2,1)S(1)} %copy-done, bf16[32,128,256]{2,1,0:T(8,128)(2,1)S(1)} %bitcast.62), kind=kOutput, calls=%fused_computation.10 | convolution fusion | flops 1073741824 | bytes 23068672 | tf_op jit(solution)/shard_map/skij,sih->skjh/dot_general | solution.py:69
  277.6 17.7 %copy.51 = f32[128,128,256]{2,0,1:T(8,128)} copy(f32[128,128,256]{1,2,0:T(8,128)} %bitcast.57) | data formatting | bytes 33554432 | tf_op jit(solution)/shard_map/reshape | solution.py:73
  295.3 9.0 %convolution_convert_fusion.4 = bf16[4,128,256]{2,0,1:T(4,128)(2,1)S(1)} fusion(f32[128,128,256]{2,0,1:T(8,128)} %copy.51, s32[128]{0:T(128)S(1)} %eq.67), kind=kOutput, calls=%fused_computation.15 | convolution fusion | flops 201458176 | bytes 17039872 | tf_op jit(solution)/shard_map/bn,njh->bjh/dot_general | solution.py:74
  304.4 2.1 convolution_bitcast_fusion
  306.5 29.8 %reduce-scatter.2.cloned.1.call-done = f32[256,512]{0,1:T(8,128)} async-done(((f32[1024,512]{0,1:T(8,128)}), f32[256,512]{0,1:T(8,128)}) %reduce-scatter.2.cloned.1.call-update) | async-done | bytes 524304 | tf_op jit(solution)/shard_map/reduce_scatter | solution.py:79
  337.8 12.2 %collective-permute-done = f32[256,512]{0,1:T(8,128)S(1)} collective-permute-done((f32[256,512]{0,1:T(8,128)}, f32[256,512]{0,1:T(8,128)S(1)}, u32[]{:S(2)}, u32[]{:S(2)}) %collective-permute-start) | collective-permute-done | bytes 524320 | tf_op jit(solution)/shard_map/ppermute | solution.py:89
  352.6 11.2 %collective-permute-done.1 = f32[256,512]{0,1:T(8,128)S(1)} collective-permute-done((f32[256,512]{0,1:T(8,128)S(1)}, f32[256,512]{0,1:T(8,128)S(1)}, u32[]{:S(2)}, u32[]{:S(2)}) %collective-permute-start.1) | collective-permute-done | bytes 524320 | tf_op jit(solution)/shard_map/ppermute | solution.py:89
  363.9 2.5 collective-permute-start.2
  366.4 21.5 %collective-permute-done.2 = f32[256,512]{0,1:T(8,128)S(1)} collective-permute-done((f32[256,512]{0,1:T(8,128)S(1)}, f32[256,512]{0,1:T(8,128)S(1)}, u32[]{:S(2)}, u32[]{:S(2)}) %collective-permute-start.2) | collective-permute-done | bytes 524320 | tf_op jit(solution)/shard_map/ppermute | solution.py:89
  (49 shorter events, 15.0 us)
Async XLA Ops:
  7.2 32.2 %all-gather.2.cloned.1.call-start = ((), (), s32[]{:S(2)}) async-start(), calls=%async_computation.5 | async-start | bytes 1310720 | tf_op jit(solution)/shard_map/all_gather | solution.py:18
  7.9 24.1 %all-to-all-start.1 = ((bf16[4,512,256]{2,1,0:T(8,128)(2,1)}), bf16[4,512,256]{2,1,0:T(8,128)(2,1)S(1)}, u32[]{:S(2)}, u32[]{:S(2)}) async-start(bf16[4,512,256]{2,1,0:T(8,128)(2,1)} %bitcast.67), calls=%async_computation.1 | async-start | bytes 2097152 | tf_op jit(solution)/shard_map/all_to_all | solution.py:17
  32.0 30.6 %all-to-all-start = ((s32[8,1,8]{2,1,0:T(1,128)}), s32[8,1,8]{2,1,0:T(1,128)S(1)}, u32[]{:S(2)}, u32[]{:S(2)}) async-start(s32[8,1,8]{2,1,0:T(1,128)} %bitcast.2), calls=%async_computation | async-start | bytes 8192 | tf_op jit(solution)/shard_map/all_to_all | solution.py:44
  41.3 6.5 %copy-start.1 = (bf16[512,512]{1,0:T(8,128)(2,1)}, bf16[512,512]{1,0:T(8,128)(2,1)S(1)}, u32[]{:S(2)}) copy-start(bf16[512,512]{1,0:T(8,128)(2,1)S(1)} %convolution_convert_fusion.3) | copy-start | bytes 1572868
  62.6 6.2 %copy-start.5 = (s32[512]{0:T(512)S(1)}, s32[512]{0:T(512)}, u32[]{:S(2)}) copy-start(s32[512]{0:T(512)} %param.14) | copy-start | bytes 6148
  62.6 98.2 %all-to-all-start.2 = ((bf16[8,8,32768]{2,1,0:T(8,128)(2,1)}), bf16[8,8,32768]{2,1,0:T(8,128)(2,1)}, u32[]{:S(2)}, u32[]{:S(2)}) async-start(bf16[8,8,32768]{2,1,0:T(8,128)(2,1)} %fusion), calls=%async_computation.2 | async-start | bytes 8388608 | tf_op jit(solution)/shard_map/all_to_all | solution.py:43
  68.8 95.2 %copy-start.2 = (bf16[512,512]{1,0:T(8,128)(2,1)S(1)}, bf16[512,512]{1,0:T(8,128)(2,1)}, u32[]{:S(2)}) copy-start(bf16[512,512]{1,0:T(8,128)(2,1)} %copy-done.1) | copy-start | bytes 1572868
  68.8 95.2 %copy-start.3 = (bf16[512,256]{1,0:T(8,128)(2,1)S(1)}, bf16[512,256]{1,0:T(8,128)(2,1)}, u32[]{:S(2)}) copy-start(bf16[512,256]{1,0:T(8,128)(2,1)} %param.15) | copy-start | bytes 786436
  168.6 4.9 %copy-start.4 = (s32[32,4]{0,1:T(4,128)S(1)}, s32[32,4]{0,1:T(4,128)}, u32[]{:S(2)}) copy-start(s32[32,4]{0,1:T(4,128)} %param.13) | copy-start | bytes 1540
  168.6 97.2 %all-to-all-start.3 = ((bf16[8,8,32768]{2,1,0:T(8,128)(2,1)}), bf16[8,8,32768]{2,1,0:T(8,128)(2,1)}, u32[]{:S(2)}, u32[]{:S(2)}) async-start(bf16[8,8,32768]{2,1,0:T(8,128)(2,1)} %fusion.1), calls=%async_computation.3 | async-start | bytes 8388608 | tf_op jit(solution)/shard_map/all_to_all | solution.py:62
  173.3 163.0 %reduce-scatter.2.cloned.1.call-start = ((), (), s32[]{:S(2)}) async-start(), calls=%async_computation.6 | async-start | bytes 2621440 | tf_op jit(solution)/shard_map/reduce_scatter | solution.py:79
  265.9 3.6 copy-start
  336.3 13.7 %collective-permute-start = (f32[256,512]{0,1:T(8,128)}, f32[256,512]{0,1:T(8,128)S(1)}, u32[]{:S(2)}, u32[]{:S(2)}) collective-permute-start(f32[256,512]{0,1:T(8,128)} %reduce-scatter.2.cloned.1.call-done), channel_id=1, source_target_pairs={{0,4},{4,0},{8,12},{12,8},{16,20},{20,16},{24,28},{28,24},{1,5},{5... | collective-permute-start | bytes 1572872 | tf_op jit(solution)/shard_map/ppermute | solution.py:89
  351.1 12.7 %collective-permute-start.1 = (f32[256,512]{0,1:T(8,128)S(1)}, f32[256,512]{0,1:T(8,128)S(1)}, u32[]{:S(2)}, u32[]{:S(2)}) collective-permute-start(f32[256,512]{0,1:T(8,128)S(1)} %add.65), channel_id=1, source_target_pairs={{0,8},{4,12},{8,0},{12,4},{16,24},{20,28},{24,16},{28,20},{1,9},{5... | collective-permute-start | bytes 1572872 | tf_op jit(solution)/shard_map/ppermute | solution.py:89
  363.9 24.0 %collective-permute-start.2 = (f32[256,512]{0,1:T(8,128)S(1)}, f32[256,512]{0,1:T(8,128)S(1)}, u32[]{:S(2)}, u32[]{:S(2)}) collective-permute-start(f32[256,512]{0,1:T(8,128)S(1)} %add.66), channel_id=1, source_target_pairs={{0,16},{4,20},{8,24},{12,28},{16,0},{20,4},{24,8},{28,12},{1,17},{... | collective-permute-start | bytes 1572872 | tf_op jit(solution)/shard_map/ppermute | solution.py:89
Sparse Core Ops, SparseCore 0:
  9.5 24.1 all-gather.1
  306.6 29.6 reduce-scatter.1
